TPU v7x, 32 devices: a whole 2x2x4 slice. The times are simulated.
32 devices in a mesh: grp: 4 (over z), dev: 8 (over y, x, core).
Axes of the slice: x: 2, y: 2, z: 4, core: 2. Of those that a mesh axis runs over, the one named last changes fastest.
Arguments:
- integrals: bfloat16 [8, 1280, 1280], P('grp', 'dev'), may hold values from -0.15625 to 0.15625
- amplitudes: bfloat16 [8, 1280, 4, 192], P(None, 'grp', None, 'dev'), may hold values from -6 to 6
- occupied_energy: float32 [40], replicated, may hold values from -1.5 to -0.3
- virtual_energy: float32 [280], replicated, may hold values from 0.2 to 3
- virtual_pairs: int32 [8, 1280, 2], P('grp', 'dev'), may hold values from 0 to 279
- occupied_pairs: int32 [192, 2], replicated, may hold values from 0 to 39
Outputs:
- update: bfloat16 [8, 1280, 4, 192], P(None, 'dev', None, 'grp')
All inputs are finite; a program needn't handle non-finite values.
Results may differ from a plain program's by a relative error of at most 0.001.
Values may be sent and summed in bfloat16 or wider, within the bound.
A program may use at most 64 MiB of HBM per device.

v0:
```python
import functools

import jax
import jax.numpy as jnp
from jax import lax
from jax.experimental import pallas as pl
from jax.experimental.pallas import tpu as pltpu
from jax.sharding import PartitionSpec as P

LANES = 128
F32 = jnp.float32
BF16 = jnp.bfloat16


def lookup(energy, indices):
    labels = jnp.arange(energy.shape[0], dtype=jnp.int32)
    picked = indices[:, None] == labels[None, :]
    return jnp.sum(jnp.where(picked, energy[None, :], 0.0), axis=1)


def plain(integrals, amplitudes, occupied_energy, virtual_energy, virtual_pairs, occupied_pairs):
    arrived = lax.all_to_all(amplitudes, "grp", split_axis=0, concat_axis=1, tiled=True)
    occ_sum = lookup(occupied_energy, occupied_pairs[:, 0]) + lookup(
        occupied_energy, occupied_pairs[:, 1]
    )
    results = []
    for block in range(arrived.shape[0]):
        panel = arrived[block]
        block_ints = integrals[block]
        gathered = lax.all_gather(panel, "dev", axis=2, tiled=True)
        ladder = jnp.einsum("ae,evj->avj", block_ints, gathered, preferred_element_type=jnp.float32)
        pairs_here = virtual_pairs[block]
        virt_sum = lookup(virtual_energy, pairs_here[:, 0]) + lookup(
            virtual_energy, pairs_here[:, 1]
        )
        denominator = occ_sum[None, :] - virt_sum[:, None]
        results.append((ladder / denominator[:, None, :]).astype(jnp.bfloat16))
    stacked = jnp.stack(results)
    return lax.all_to_all(stacked, "grp", split_axis=3, concat_axis=0, tiled=True)


def as_column(row):
    n = row.shape[1]
    eye = lax.broadcasted_iota(jnp.int32, (n, n), 0) == lax.broadcasted_iota(jnp.int32, (n, n), 1)
    return jnp.sum(jnp.where(eye, jnp.broadcast_to(row, (n, n)), 0.0), axis=1, keepdims=True)


def picked_row(column, index_row):
    shape = (column.shape[0], index_row.shape[1])
    hit = lax.broadcasted_iota(jnp.int32, shape, 0) == jnp.broadcast_to(index_row, shape)
    return jnp.sum(jnp.where(hit, jnp.broadcast_to(column, shape), 0.0), axis=0, keepdims=True)


def body(
    dims,
    ints_hbm,
    amps_hbm,
    occ_e_hbm,
    virt_e_hbm,
    vpairs_hbm,
    opairs_hbm,
    out,
    ints,
    amps,
    occ_e,
    virt_e,
    vpairs,
    opairs,
    packed,
    gath,
    other_ints,
    other_pairs,
    weights,
    recip,
    occ_col,
    sendbuf,
    recvbuf,
    z_send,
    z_recv,
    xy_send,
    xy_recv,
    o_send,
    o_recv,
    pair_send,
    pair_recv,
    load_amps,
    load_rest,
):
    groups, blocks_here, vec, nij, nab, nef = dims
    rows = vec * nij
    half = rows // 2
    tail = nef % LANES
    chunk = packed.shape[1]
    cut = chunk // 32 * 16
    z = lax.axis_index("grp")
    dev = lax.axis_index("dev")
    core = dev % 2
    chip = dev // 2
    flip_x = chip + 1 - 2 * (chip % 2)
    flip_y = chip + 2 - 4 * (chip // 2)
    mesh_id = pl.DeviceIdType.MESH

    def at(zz, pp, cc):
        return (zz, pp * 2 + cc)

    low = z < groups // 2

    def far(step):
        down = groups - 1 - step
        down = down - jnp.where(down <= z, 1, 0)
        up = step + jnp.where(step >= z, 1, 0)
        return jnp.where(low, down, up)

    barrier = pltpu.get_barrier_semaphore()
    peers = [at(z, chip, 1 - core), at(z, flip_x, core), at(z, flip_y, core)]
    for s in range(groups - 1):
        peers.append(at(far(s), chip, core))
        peers.append(at(far(s), chip, 1 - core))
    for peer in peers:
        pl.semaphore_signal(barrier, inc=1, device_id=peer, device_id_type=mesh_id)

    loads = []
    for blk in range(packed.shape[0]):
        loads.append(pltpu.make_async_copy(amps_hbm.at[blk], amps.at[blk], load_amps.at[blk]))
    pairs = [(ints_hbm, ints), (occ_e_hbm, occ_e), (virt_e_hbm, virt_e), (vpairs_hbm, vpairs), (opairs_hbm, opairs)]
    rest = [pltpu.make_async_copy(src, dst, load_rest.at[i]) for i, (src, dst) in enumerate(pairs)]
    for load in loads + rest:
        load.start()

    for blk in range(packed.shape[0]):
        loads[blk].wait()
        packed[blk, 0:rows, :] = amps[blk, :, 0:LANES]
        packed[blk, rows : 2 * rows, :] = amps[blk, :, LANES : 2 * LANES]
        left = amps[blk, 0:half, 2 * LANES : nef].astype(F32)
        right = amps[blk, half:rows, 2 * LANES : nef].astype(F32)
        packed[blk, 2 * rows : chunk, :] = jnp.concatenate([left, right], axis=1).astype(BF16)

    pl.semaphore_wait(barrier, len(peers))

    started = []

    def send(src, dst, ssem, rsem, to):
        copy = pltpu.make_async_remote_copy(
            src_ref=src, dst_ref=dst, send_sem=ssem, recv_sem=rsem, device_id=to, device_id_type=mesh_id
        )
        copy.start()
        started.append(copy)
        return copy

    for b in range(blocks_here):
        for s in range(groups - 1):
            to = far(s)
            send(
                packed.at[to * blocks_here + b],
                gath.at[b, z, chip],
                z_send.at[b, s],
                z_recv.at[b, z],
                at(to, chip, core),
            )

    def arrived(ref, sem):
        pltpu.make_async_remote_copy(
            src_ref=ref, dst_ref=ref, send_sem=sem, recv_sem=sem,
            device_id=at(z, chip, 1 - core), device_id_type=mesh_id,
        ).wait_recv()

    order = [(b, None) for b in range(blocks_here)]
    order += [(b, s) for b in range(blocks_here) for s in range(groups - 1)]

    def source(s):
        return z if s is None else far(s)

    def first(k):
        b, s = order[k]
        zz = source(s)
        src = gath.at[b, zz, chip]
        if s is None:
            src = packed.at[z * blocks_here + b]
        else:
            arrived(src, z_recv.at[b, zz])
        send(src, gath.at[b, zz, chip], xy_send.at[k, 0], xy_recv.at[b, zz, 0], at(z, flip_x, core))
        send(src, gath.at[b, zz, chip], xy_send.at[k, 1], xy_recv.at[b, zz, 1], at(z, flip_y, core))

    def second(k):
        b, s = order[k]
        zz = source(s)
        arrived(gath.at[b, zz, flip_x], xy_recv.at[b, zz, 0])
        src = gath.at[b, zz, flip_x, 0:cut]
        send(src, src, xy_send.at[k, 2], xy_recv.at[b, zz, 2], at(z, flip_y, core))
        arrived(gath.at[b, zz, flip_y], xy_recv.at[b, zz, 1])
        src = gath.at[b, zz, flip_y, cut:chunk]
        send(src, src, xy_send.at[k, 3], xy_recv.at[b, zz, 3], at(z, flip_x, core))

    def third(k):
        b, s = order[k]
        zz = source(s)
        diag = 3 - chip
        arrived(gath.at[b, zz, diag, 0:cut], xy_recv.at[b, zz, 2])
        arrived(gath.at[b, zz, diag, cut:chunk], xy_recv.at[b, zz, 3])

    for k in range(blocks_here):
        first(k)
    partner = at(z, chip, 1 - core)
    for load in rest:
        load.wait()
    send(vpairs, other_pairs, pair_send.at[0], pair_recv.at[0], partner)
    send(ints, other_ints, pair_send.at[1], pair_recv.at[1], partner)

    for b in range(blocks_here):
        gath[b, z, chip] = packed[z * blocks_here + b]

    occ_column = as_column(occ_e[...].reshape(1, -1))
    occ_row = picked_row(occ_column, opairs[0:1, :]) + picked_row(occ_column, opairs[1:2, :])
    occ_col[...] = jnp.broadcast_to(as_column(occ_row), occ_col.shape)
    virt_column = as_column(virt_e[...].reshape(1, -1))

    def prepare(side, int_ref, pair_ref):
        for b in range(blocks_here):
            virt_row = picked_row(virt_column, pair_ref[b, 0:1, :]) + picked_row(
                virt_column, pair_ref[b, 1:2, :]
            )
            for p in range(gath.shape[2]):
                start = pl.multiple_of((2 * p + core) * nij, 8)
                occ = occ_col[pl.ds(start, nij), 0:1]
                recip[b, side, p] = 1.0 / (occ - virt_row)
            for zz in range(groups):
                panel = int_ref[b, :, zz * nef : (zz + 1) * nef].astype(F32)
                last = panel[:, 2 * LANES : nef]
                wide = jnp.concatenate([panel[:, 0 : 2 * LANES], last, last], axis=1)
                width = 3 * LANES
                weights[b, side, :, zz * width : (zz + 1) * width] = wide.astype(BF16)

    second(0)
    prepare(0, ints, vpairs)
    later = blocks_here
    first(later)
    second(1)
    first(later + 1)
    arrived(other_pairs, pair_recv.at[0])
    arrived(other_ints, pair_recv.at[1])
    prepare(1, other_ints, other_pairs)

    chips = gath.shape[2]
    lane = lax.broadcasted_iota(jnp.int32, (half, LANES), 1)
    main_lanes = nab // LANES * LANES

    def compute(b):
        parts = []
        for zz in range(groups):
            per_chip = []
            for p in range(chips):
                end = gath[b, zz, p, 2 * rows : chunk, :]
                zero = jnp.zeros_like(end)
                end2 = jnp.concatenate(
                    [jnp.where(lane < tail, end, zero), jnp.where(lane < tail, zero, end)], axis=0
                )
                per_chip.append(
                    jnp.concatenate([gath[b, zz, p, 0:rows, :], gath[b, zz, p, rows : 2 * rows, :], end2], axis=1)
                )
            parts.append(jnp.concatenate(per_chip, axis=0))
        left = jnp.concatenate(parts, axis=1)
        for side in range(2):
            total = lax.dot_general(
                left, weights[b, side], (((1,), (1,)), ((), ())), preferred_element_type=F32
            )
            scaled = total.reshape(chips, vec, nij, nab) * recip[b, side][:, None]
            to_core = jnp.where(side == 0, core, 1 - core)
            for p in range(chips):
                ends = [scaled[p, v, :, main_lanes:nab] for v in range(vec)]
                sendbuf[b, p, side, 0:rows, :] = scaled[p, :, :, 0:main_lanes].reshape(rows, main_lanes).astype(BF16)
                sendbuf[b, p, side, rows : rows + nij, :] = jnp.concatenate(ends, axis=1).astype(BF16)
        for s in range(groups - 1):
            to = far(s)
            for side in range(2):
                send(
                    sendbuf.at[b, to, side], recvbuf.at[z, b, core],
                    o_send.at[b, s, side], o_recv.at[z, b, core],
                    at(to, chip, core if side == 0 else 1 - core),
                )
        send(
            sendbuf.at[b, z, 1], recvbuf.at[z, b, core],
            o_send.at[b, groups - 1, 1], o_recv.at[z, b, core], partner,
        )
        recvbuf[z, b, core] = sendbuf[b, z, 0]

    def unpack(zz, b):
        got = [recvbuf[zz, b, c].astype(F32) for c in range(2)]
        width = nab - main_lanes
        for v in range(vec):
            pieces = []
            for c in range(2):
                main = got[c][v * nij : (v + 1) * nij, :]
                end = got[c][rows : rows + nij, v * width : (v + 1) * width]
                pieces.append(jnp.concatenate([main, end], axis=1))
            out[zz * blocks_here + b, v] = jnp.concatenate(pieces, axis=0).astype(BF16)

    steps = len(order)
    per = groups - 1
    first(later + 2)
    pos = later + 3
    done = 2
    ready = {b: later + (b + 1) * per for b in range(blocks_here)}
    for b in range(blocks_here):
        while done < ready[b]:
            if pos < steps:
                first(pos)
                pos += 1
            second(done)
            done += 1
        third(b)
        for k in range(later + b * per, later + (b + 1) * per):
            third(k)
        compute(b)

    for b in range(blocks_here):
        arrived(recvbuf.at[z, b, 1 - core], o_recv.at[z, b, 1 - core])
        unpack(z, b)
        for s in range(groups - 1):
            zz = far(s)
            for c in range(2):
                arrived(recvbuf.at[zz, b, c], o_recv.at[zz, b, c])
            unpack(zz, b)
    for copy in started:
        copy.wait_send()


def fused(groups, integrals, amplitudes, occupied_energy, virtual_energy, virtual_pairs, occupied_pairs):
    nblk, nef, vec, nij = amplitudes.shape
    here, nab, _ = integrals.shape
    rows = vec * nij
    chips = lax.axis_size("dev") // 2
    amps = jnp.transpose(amplitudes, (0, 2, 3, 1)).reshape(nblk, rows, nef)
    vpairs = jnp.transpose(virtual_pairs, (0, 2, 1))
    opairs = jnp.transpose(occupied_pairs, (1, 0))
    chunk = 2 * rows + rows // 2
    dims = (groups, here, vec, nij, nab, nef)
    dma = pltpu.SemaphoreType.DMA
    nchunks = here * groups
    result = pl.pallas_call(
        functools.partial(body, dims),
        out_shape=jax.ShapeDtypeStruct((nblk, vec, 2 * nij, nab), BF16),
        in_specs=[pl.BlockSpec(memory_space=pltpu.HBM)] * 6,
        out_specs=pl.BlockSpec(memory_space=pltpu.VMEM),
        scratch_shapes=[
            pltpu.VMEM(integrals.shape, BF16),
            pltpu.VMEM(amps.shape, BF16),
            pltpu.VMEM(occupied_energy.shape, F32),
            pltpu.VMEM(virtual_energy.shape, F32),
            pltpu.VMEM(vpairs.shape, jnp.int32),
            pltpu.VMEM(opairs.shape, jnp.int32),
            pltpu.VMEM((nblk, chunk, LANES), BF16),
            pltpu.VMEM((here, groups, chips, chunk, LANES), BF16),
            pltpu.VMEM(integrals.shape, BF16),
            pltpu.VMEM(vpairs.shape, jnp.int32),
            pltpu.VMEM((here, 2, nab, groups * 3 * LANES), BF16),
            pltpu.VMEM((here, 2, chips, nij, nab), F32),
            pltpu.VMEM((2 * chips * nij, LANES), F32),
            pltpu.VMEM((here, groups, 2, rows + nij, LANES), BF16),
            pltpu.VMEM((groups, here, 2, rows + nij, LANES), BF16),
            dma((here, groups - 1)),
            dma((here, groups)),
            dma((nchunks, 4)),
            dma((here, groups, 4)),
            dma((here, groups, 2)),
            dma((groups, here, 2)),
            dma((2,)),
            dma((2,)),
            dma((nblk,)),
            dma((5,)),
        ],
        compiler_params=pltpu.CompilerParams(
            collective_id=0, has_side_effects=True, vmem_limit_bytes=67_043_328
        ),
        name="ladder",
    )(
        integrals,
        amps,
        occupied_energy,
        virtual_energy,
        vpairs,
        opairs,
    )
    return jnp.transpose(result, (0, 3, 1, 2))


def solution(mesh):
    placed = (
        P("grp", "dev", None),
        P(None, "grp", None, "dev"),
        P(),
        P(),
        P("grp", "dev", None),
        P(),
    )
    groups, devs = mesh.shape["grp"], mesh.shape["dev"]

    def local(integrals, amplitudes, *rest):
        nef, vec, nij = amplitudes.shape[1:]
        nab = integrals.shape[1]
        square = devs == 2 * 2 * 2 and devs == 2 * groups
        packs = (
            2 * LANES < nef < 3 * LANES
            and 2 * (nef % LANES) == LANES
            and LANES < nab < 2 * LANES
            and vec * (nab % LANES) == LANES
            and nij % 8 == 0
            and (vec * nij) % 32 == 0
        )
        if square and packs:
            return fused(groups, integrals, amplitudes, *rest)
        return plain(integrals, amplitudes, *rest)

    return jax.shard_map(
        local, mesh=mesh, in_specs=placed, out_specs=P(None, "dev", None, "grp"), check_vma=False
    )
```

profile of v0, /device:TPU:0, one launch (start us, length us, event | category | flops | bytes accessed | tf_op | source)
XLA Modules:
  0.0 38.5 jit_solution(7227863351116093461)
XLA Ops:
  0.0 36.4 %ladder.1 = bf16[8,4,48,160]{3,2,1,0:T(8,128)(2,1)} custom-call(bf16[2,160,1280]{2,1,0:T(8,128)(2,1)} %ints_hbm.1, bf16[8,96,320]{2,1,0:T(8,128)(2,1)} %bitcast.7, f32[40]{0:T(128)} %occ_e_hbm.1, f32[280]{0:T(512)} %virt_e_hbm.1, s32[2,2,160]{2,1,0:T(2,128)} %bitcast.8, s32[2,192]{1,0:T(2,128)} %bitcast.9), custom_call_target="tpu_custom_call" | custom-call | tf_op jit(solution)/shard_map/ladder/pallas_call | solution.py:339
  36.4 2.1 %copy.8 = bf16[8,160,4,48]{1,3,2,0:T(8,128)(2,1)} copy(bf16[8,160,4,48]{1,3,2,0:T(8,128)(2,1)} %bitcast.6) | data formatting | bytes 983040
where the time goes:
time: 38.7 us; the launch traced here: 38.5 us
  Pallas kernels  36.4 us (94%)
  local copies, waits for them, and re-layouts  2.06 us (5%)
    pallas_call x1, Pallas kernels, fused(): pl.pallas_call(functools.partial(body, dims), out_shape=jax.ShapeDtypeStr...  36.4 us
    unnamed x1, local copies, waits for them, and re-layouts  2.06 us

commit v1 on v0

--- a/solution.py
+++ b/solution.py
@@ -336,6 +336,7 @@
     dims = (groups, here, vec, nij, nab, nef)
     dma = pltpu.SemaphoreType.DMA
     nchunks = here * groups
+    arrays = (integrals, amps, occupied_energy, virtual_energy, vpairs, opairs)
     result = pl.pallas_call(
         functools.partial(body, dims),
         out_shape=jax.ShapeDtypeStruct((nblk, vec, 2 * nij, nab), BF16),
@@ -369,17 +370,10 @@
             dma((5,)),
         ],
         compiler_params=pltpu.CompilerParams(
-            collective_id=0, has_side_effects=True, vmem_limit_bytes=67_043_328
+            collective_id=0, has_side_effects=True, vmem_limit_bytes=32 * 1024 * 1024
         ),
         name="ladder",
-    )(
-        integrals,
-        amps,
-        occupied_energy,
-        virtual_energy,
-        vpairs,
-        opairs,
-    )
+    )(*[pltpu.with_memory_space_constraint(array, pltpu.HBM) for array in arrays])
     return jnp.transpose(result, (0, 3, 1, 2))
 
 

time: 38.7 us -> 36.6 us (0.946)
  local copies, waits for them, and re-layouts: 2.06 us -> 0.88 us
  Pallas kernels: 36.4 us -> 35.5 us
    unnamed x1, local copies, waits for them, and re-layouts: 2.06 us -> 0.88 us
    pallas_call x1, Pallas kernels: 36.4 us -> 35.5 us  [fused(): pl.pallas_call(functools.partial(body, dims), out_shape=jax.ShapeDtypeStr...]
where the time goes in v1:
time: 36.6 us; the launch traced here: 36.4 us
  Pallas kernels  35.5 us (97%)
  local copies, waits for them, and re-layouts  0.88 us (2%)
    pallas_call x1, Pallas kernels, fused(): pl.pallas_call(functools.partial(body, dims), out_shape=jax.ShapeDtypeStr...  35.5 us
    unnamed x1, local copies, waits for them, and re-layouts  0.88 us

profile of v1, /device:TPU:0, one launch (start us, length us, event | category | flops | bytes accessed | tf_op | source)
XLA Modules:
  0.0 36.4 jit_solution(6500787031286180494)
XLA Ops:
  0.0 35.5 %ladder.1 = bf16[8,4,48,160]{3,2,1,0:T(8,128)(2,1)S(1)} custom-call(bf16[2,160,1280]{2,1,0:T(8,128)(2,1)} %ints_hbm.1, bf16[8,96,320]{2,1,0:T(8,128)(2,1)} %bitcast.7, f32[40]{0:T(128)} %occ_e_hbm.1, f32[280]{0:T(512)} %virt_e_hbm.1, s32[2,2,160]{2,1,0:T(2,128)} %bitcast.8, s32[2,192]{1,0:T(2,128)} %bitcast.9), custom_call_target="tpu_custom_call" | custom-call | tf_op jit(solution)/shard_map/ladder/pallas_call | solution.py:340
  35.6 0.9 %copy.8 = bf16[8,160,4,48]{1,3,2,0:T(8,128)(2,1)} copy(bf16[8,160,4,48]{1,3,2,0:T(8,128)(2,1)S(1)} %bitcast.6) | data formatting | bytes 983040

commit v2 on v1

v2 whole, which is shorter than its diff:
```python
import functools

import jax
import jax.numpy as jnp
from jax import lax
from jax.experimental import pallas as pl
from jax.experimental.pallas import tpu as pltpu
from jax.sharding import PartitionSpec as P

LANES = 128
F32 = jnp.float32
BF16 = jnp.bfloat16


def lookup(energy, indices):
    labels = jnp.arange(energy.shape[0], dtype=jnp.int32)
    picked = indices[:, None] == labels[None, :]
    return jnp.sum(jnp.where(picked, energy[None, :], 0.0), axis=1)


def plain(integrals, amplitudes, occupied_energy, virtual_energy, virtual_pairs, occupied_pairs):
    arrived = lax.all_to_all(amplitudes, "grp", split_axis=0, concat_axis=1, tiled=True)
    occ_sum = lookup(occupied_energy, occupied_pairs[:, 0]) + lookup(
        occupied_energy, occupied_pairs[:, 1]
    )
    results = []
    for block in range(arrived.shape[0]):
        panel = arrived[block]
        block_ints = integrals[block]
        gathered = lax.all_gather(panel, "dev", axis=2, tiled=True)
        ladder = jnp.einsum("ae,evj->avj", block_ints, gathered, preferred_element_type=jnp.float32)
        pairs_here = virtual_pairs[block]
        virt_sum = lookup(virtual_energy, pairs_here[:, 0]) + lookup(
            virtual_energy, pairs_here[:, 1]
        )
        denominator = occ_sum[None, :] - virt_sum[:, None]
        results.append((ladder / denominator[:, None, :]).astype(jnp.bfloat16))
    stacked = jnp.stack(results)
    return lax.all_to_all(stacked, "grp", split_axis=3, concat_axis=0, tiled=True)


def as_column(row):
    n = row.shape[1]
    eye = lax.broadcasted_iota(jnp.int32, (n, n), 0) == lax.broadcasted_iota(jnp.int32, (n, n), 1)
    return jnp.sum(jnp.where(eye, jnp.broadcast_to(row, (n, n)), 0.0), axis=1, keepdims=True)


def picked_row(column, index_row):
    shape = (column.shape[0], index_row.shape[1])
    hit = lax.broadcasted_iota(jnp.int32, shape, 0) == jnp.broadcast_to(index_row, shape)
    return jnp.sum(jnp.where(hit, jnp.broadcast_to(column, shape), 0.0), axis=0, keepdims=True)


def body(
    dims,
    ints_hbm,
    amps_hbm,
    occ_e_hbm,
    virt_e_hbm,
    vpairs_hbm,
    opairs_hbm,
    out,
    ints,
    amps,
    occ_e,
    virt_e,
    vpairs,
    opairs,
    tails,
    gath,
    other_ints,
    other_pairs,
    weights,
    recip,
    occ_col,
    sendbuf,
    recvbuf,
    ready,
    z_send,
    z_recv,
    d_send,
    d_recv,
    f_send,
    f_recv,
    o_send,
    o_recv,
    pair_send,
    pair_recv,
    load_amps,
    load_own,
    load_rest,
):
    groups, blocks_here, vec, nij, nab, nef = dims
    rows = vec * nij
    half = rows // 2
    tail = nef % LANES
    main = nef - tail
    bulk = main // LANES * rows
    chunk = bulk + half
    cut = chunk // 32 * 16
    z = lax.axis_index("grp")
    dev = lax.axis_index("dev")
    core = dev % 2
    chip = dev // 2
    flip_x = chip + 1 - 2 * (chip % 2)
    flip_y = chip + 2 - 4 * (chip // 2)
    diag = 3 - chip
    mesh_id = pl.DeviceIdType.MESH

    def at(zz, pp, cc):
        return (zz, pp * 2 + cc)

    low = z < groups // 2

    def far(step):
        down = groups - 1 - step
        down = down - jnp.where(down <= z, 1, 0)
        up = step + jnp.where(step >= z, 1, 0)
        return jnp.where(low, down, up)

    def across(step):
        return jnp.where(low, groups // 2 + step, groups // 2 - 1 - step)

    def reach(step):
        return jnp.where(step < z, z - 1 - step, step + 1)

    loads = []
    for b in range(blocks_here):
        loads.append(pltpu.make_async_copy(amps_hbm.at[z * blocks_here + b], amps.at[b], load_amps.at[0]))
    for s in range(groups - 1):
        for b in range(blocks_here):
            slot = (s + 1) * blocks_here + b
            loads.append(
                pltpu.make_async_copy(amps_hbm.at[reach(s) * blocks_here + b], amps.at[slot], load_amps.at[1])
            )

    def bulk_parts(block, piece):
        for i in range(main // LANES):
            yield amps_hbm.at[block, :, i * LANES : (i + 1) * LANES], piece.at[i * rows : (i + 1) * rows]

    for b in range(blocks_here):
        for src, dst in bulk_parts(z * blocks_here + b, gath.at[b, z, chip]):
            loads.append(pltpu.make_async_copy(src, dst, load_own.at[0]))
    pairs = [(ints_hbm, ints), (occ_e_hbm, occ_e), (virt_e_hbm, virt_e), (vpairs_hbm, vpairs), (opairs_hbm, opairs)]
    rest = [pltpu.make_async_copy(src, dst, load_rest.at[i]) for i, (src, dst) in enumerate(pairs)]

    partner = at(z, chip, 1 - core)
    x_peer = at(z, flip_x, core)
    y_peer = at(z, flip_y, core)
    swap = chip == 2
    ways = [
        at(z, jnp.where(swap, flip_y, flip_x), core),
        at(z, jnp.where(swap, flip_x, flip_y), core),
    ]
    peers = [(partner, core == 0, 0), (x_peer, chip % 2 == 0, 1), (y_peer, chip < 2, 2)]
    for s in range(groups - 1):
        zz = reach(s)
        for c in range(2):
            peers.append((at(zz, chip, core if c == 0 else 1 - core), zz > z, 3 + s * 2 + c))
    barrier = pltpu.get_barrier_semaphore()
    for peer, higher, _ in peers:
        @pl.when(higher)
        def _(peer=peer):
            pl.semaphore_signal(barrier, inc=1, device_id=peer, device_id_type=mesh_id)
    for load in loads + rest:
        load.start()
    earlier = 2 * z + chip % 2 + chip // 2 + core

    @pl.when(earlier > 0)
    def _():
        pl.semaphore_wait(barrier, earlier)

    for i, (peer, higher, slot) in enumerate(peers):
        if i < 3:
            there = slot
        else:
            s, c = (i - 3) // 2, (i - 3) % 2
            zz = reach(s)
            there = 3 + c + 2 * jnp.where(z < zz, zz - 1 - z, z - 1)

        @pl.when(jnp.logical_not(higher))
        def _(peer=peer, there=there):
            pl.semaphore_signal(ready.at[there], inc=1, device_id=peer, device_id_type=mesh_id)

    def met(i):
        @pl.when(peers[i][1])
        def _():
            pl.semaphore_wait(ready.at[peers[i][2]], 1)

    def met_way(way):
        i = jnp.where(swap, 2 - way, 1 + way)
        higher = jnp.where(i == 1, chip % 2 == 0, chip < 2)

        @pl.when(higher)
        def _():
            pl.semaphore_wait(ready.at[i], 1)

    def send(src, dst, ssem, rsem, to):
        pltpu.make_async_remote_copy(
            src_ref=src, dst_ref=dst, send_sem=ssem, recv_sem=rsem, device_id=to, device_id_type=mesh_id
        ).start()

    def whole(ref, sem):
        return pltpu.make_async_remote_copy(
            src_ref=ref, dst_ref=ref, send_sem=sem, recv_sem=sem, device_id=partner, device_id_type=mesh_id
        )

    def arrived(ref, sem):
        whole(ref, sem).wait_recv()

    def left(ref, sem):
        whole(ref, sem).wait_send()

    order = [(b, s) for s in (0, 1) for b in range(blocks_here)]
    order += [(b, s) for b in range(blocks_here) for s in range(2, groups)]

    def source(s):
        if s < 2:
            return z if s == 0 else z + 1 - 2 * (z % 2)
        return across(s - 2)

    def direct_main(b, way):
        for src, dst in bulk_parts(z * blocks_here + b, gath.at[b, z, chip]):
            send(src, dst, d_send.at[0], d_recv.at[b, z], ways[way])

    def direct_tail(b, way):
        send(tails.at[b], gath.at[b, z, chip, bulk:chunk], d_send.at[0], d_recv.at[b, z], ways[way])

    def inward_main(b, s):
        to = reach(s)
        for src, dst in bulk_parts(to * blocks_here + b, gath.at[b, z, chip]):
            send(src, dst, z_send.at[0], z_recv.at[b, z], at(to, chip, core))

    def inward_tail(b, s):
        to = reach(s)
        send(
            tails.at[(s + 1) * blocks_here + b], gath.at[b, z, chip, bulk:chunk],
            z_send.at[0], z_recv.at[b, z], at(to, chip, core),
        )

    def first(k):
        b, s = order[k]
        zz = source(s)
        piece = gath.at[b, zz, chip]
        arrived(piece, z_recv.at[b, zz])
        for peer in (x_peer, y_peer):
            send(piece, piece, d_send.at[0], d_recv.at[b, zz], peer)

    def second(k):
        b, s = order[k]
        zz = source(s)
        arrived(gath.at[b, zz, 0:2], d_recv.at[b, zz])
        src = gath.at[b, zz, flip_x, 0:cut]
        send(src, src, f_send.at[0], f_recv.at[b], y_peer)
        src = gath.at[b, zz, flip_y, cut:chunk]
        send(src, src, f_send.at[0], f_recv.at[b], x_peer)

    def third(b):
        arrived(gath.at[b, :, diag], f_recv.at[b])

    def pack(slot):
        lower = amps[slot, 0:half, main:nef].astype(F32)
        upper = amps[slot, half:rows, main:nef].astype(F32)
        tails[slot] = jnp.concatenate([lower, upper], axis=1).astype(BF16)

    def loaded(slots, sem):
        pltpu.make_async_copy(amps.at[slots], amps.at[slots], sem).wait()

    met_way(0)
    direct_main(0, 0)
    met_way(1)
    direct_main(0, 1)
    met(3)
    inward_main(0, 0)
    loaded(slice(0, blocks_here), load_amps.at[0])
    for b in range(blocks_here):
        pack(b)
    for b in range(blocks_here):
        if b > 0:
            direct_main(b, 0)
            direct_main(b, 1)
        direct_tail(b, 0)
        direct_tail(b, 1)
    loaded(slice(blocks_here, groups * blocks_here), load_amps.at[1])
    for slot in range(blocks_here, groups * blocks_here):
        pack(slot)
    inward_tail(0, 0)
    for s in range(1, groups - 1):
        met(3 + 2 * s)
        inward_main(0, s)
        inward_tail(0, s)
    for b in range(1, blocks_here):
        for s in range(groups - 1):
            inward_main(b, s)
            inward_tail(b, s)
    met(0)
    send(vpairs_hbm, other_pairs, pair_send.at[0], pair_recv.at[0], partner)
    send(ints_hbm, other_ints, pair_send.at[1], pair_recv.at[1], partner)
    for b in range(blocks_here):
        gath[b, z, chip, bulk:chunk] = tails[b]
    for load in rest:
        load.wait()

    occ_column = as_column(occ_e[...].reshape(1, -1))
    occ_row = picked_row(occ_column, opairs[0:1, :]) + picked_row(occ_column, opairs[1:2, :])
    occ_col[...] = jnp.broadcast_to(as_column(occ_row), occ_col.shape)
    virt_column = as_column(virt_e[...].reshape(1, -1))

    def prepare(side, int_ref, pair_ref):
        for b in range(blocks_here):
            virt_row = picked_row(virt_column, pair_ref[b, 0:1, :]) + picked_row(
                virt_column, pair_ref[b, 1:2, :]
            )
            for p in range(gath.shape[2]):
                start = pl.multiple_of((2 * p + core) * nij, 8)
                occ = occ_col[pl.ds(start, nij), 0:1]
                recip[b, side, p] = 1.0 / (occ - virt_row)
            for zz in range(groups):
                panel = int_ref[b, :, zz * nef : (zz + 1) * nef].astype(F32)
                last = panel[:, main:nef]
                wide = jnp.concatenate([panel[:, 0:main], last, last], axis=1)
                width = main + LANES
                weights[b, side, :, zz * width : (zz + 1) * width] = wide.astype(BF16)

    lane = lax.broadcasted_iota(jnp.int32, (half, LANES), 1)
    main_lanes = nab // LANES * LANES

    def job(b, p):
        parts = []
        for zz in range(groups):
            end = gath[b, zz, p, bulk:chunk]
            zero = jnp.zeros_like(end)
            end2 = jnp.concatenate(
                [jnp.where(lane < tail, end, zero), jnp.where(lane < tail, zero, end)], axis=0
            )
            parts += [gath[b, zz, p, i * rows : (i + 1) * rows] for i in range(main // LANES)] + [end2]
        panel = jnp.concatenate(parts, axis=1)
        for side in range(2):
            total = lax.dot_general(
                panel, weights[b, side], (((1,), (1,)), ((), ())), preferred_element_type=F32
            )
            scaled = total.reshape(vec, nij, nab) * recip[b, side, p][None]
            ends = [scaled[v, :, main_lanes:nab] for v in range(vec)]
            sendbuf[b, p, side, 0:rows, :] = scaled[:, :, 0:main_lanes].reshape(rows, main_lanes).astype(BF16)
            sendbuf[b, p, side, rows : rows + nij, :] = jnp.concatenate(ends, axis=1).astype(BF16)

        @pl.when(p != z)
        def _():
            for side in range(2):
                send(
                    sendbuf.at[b, p, side], recvbuf.at[z, b, core], o_send.at[0], o_recv.at[z, b],
                    at(p, chip, core if side == 0 else 1 - core),
                )

        @pl.when(p == z)
        def _():
            send(sendbuf.at[b, z, 1], recvbuf.at[z, b, core], o_send.at[1], o_recv.at[z, b], partner)
            recvbuf[z, b, core] = sendbuf[b, z, 0]

    wanted = [far(s) for s in range(groups - 1)] + [z]
    spot = sum(jnp.where(wanted[i] == diag, i, 0) for i in range(groups))
    late = [jnp.where(i >= spot, wanted[i + 1], wanted[i]) for i in range(groups - 1)] + [diag]

    def unpack(zz, b):
        got = [recvbuf[zz, b, c].astype(F32) for c in range(2)]
        width = nab - main_lanes
        for v in range(vec):
            pieces = []
            for c in range(2):
                body_rows = got[c][v * nij : (v + 1) * nij, :]
                end = got[c][rows : rows + nij, v * width : (v + 1) * width]
                pieces.append(jnp.concatenate([body_rows, end], axis=1))
            out[zz * blocks_here + b, v] = jnp.concatenate(pieces, axis=0).astype(BF16)

    prepare(0, ints, vpairs)
    second(0)
    first(2)
    second(1)
    arrived(other_pairs, pair_recv.at[0])
    arrived(other_ints, pair_recv.at[1])
    prepare(1, other_ints, other_pairs)
    first(3)
    first(4)
    second(2)
    first(5)
    second(4)
    second(5)
    pltpu.make_async_copy(gath.at[:, z, chip, 0:bulk], gath.at[:, z, chip, 0:bulk], load_own.at[0]).wait()
    for s in range(groups - 1):
        met(4 + 2 * s)
    job(0, late[0])
    job(0, late[1])
    first(6)
    job(0, late[2])
    first(7)
    second(3)
    third(0)
    job(0, late[3])
    second(6)
    second(7)
    for i in range(groups - 1):
        job(1, late[i])
    third(1)
    job(1, late[groups - 1])

    for b in range(blocks_here):
        arrived(recvbuf.at[z, b, 1 - core], o_recv.at[z, b])
        unpack(z, b)
        for s in range(groups - 1):
            zz = far(s)
            arrived(recvbuf.at[zz, b], o_recv.at[zz, b])
            unpack(zz, b)
    left(gath.at[:, 0 : groups - 1, 0], z_send.at[0])
    left(gath.at[0], d_send.at[0])
    left(gath.at[:, :, 0], f_send.at[0])
    left(sendbuf.at[:, 0 : groups - 1], o_send.at[0])
    left(sendbuf.at[:, 0, 0], o_send.at[1])
    left(other_pairs, pair_send.at[0])
    left(other_ints, pair_send.at[1])


def fused(groups, integrals, amplitudes, occupied_energy, virtual_energy, virtual_pairs, occupied_pairs):
    nblk, nef, vec, nij = amplitudes.shape
    here, nab, _ = integrals.shape
    rows = vec * nij
    chips = lax.axis_size("dev") // 2
    amps = jnp.transpose(amplitudes, (0, 2, 3, 1)).reshape(nblk, rows, nef)
    vpairs = jnp.transpose(virtual_pairs, (0, 2, 1))
    opairs = jnp.transpose(occupied_pairs, (1, 0))
    dims = (groups, here, vec, nij, nab, nef)
    dma = pltpu.SemaphoreType.DMA
    arrays = (integrals, amps, occupied_energy, virtual_energy, vpairs, opairs)
    result = pl.pallas_call(
        functools.partial(body, dims),
        out_shape=jax.ShapeDtypeStruct((nblk, vec, 2 * nij, nab), BF16),
        in_specs=[pl.BlockSpec(memory_space=pltpu.HBM)] * 6,
        out_specs=pl.BlockSpec(memory_space=pltpu.VMEM),
        scratch_shapes=[
            pltpu.VMEM(integrals.shape, BF16),
            pltpu.VMEM(amps.shape, BF16),
            pltpu.VMEM(occupied_energy.shape, F32),
            pltpu.VMEM(virtual_energy.shape, F32),
            pltpu.VMEM(vpairs.shape, jnp.int32),
            pltpu.VMEM(opairs.shape, jnp.int32),
            pltpu.VMEM((nblk, rows // 2, LANES), BF16),
            pltpu.VMEM((here, groups, chips, 2 * rows + rows // 2, LANES), BF16),
            pltpu.VMEM(integrals.shape, BF16),
            pltpu.VMEM(vpairs.shape, jnp.int32),
            pltpu.VMEM((here, 2, nab, groups * 3 * LANES), BF16),
            pltpu.VMEM((here, 2, chips, nij, nab), F32),
            pltpu.VMEM((2 * chips * nij, LANES), F32),
            pltpu.VMEM((here, groups, 2, rows + nij, LANES), BF16),
            pltpu.VMEM((groups, here, 2, rows + nij, LANES), BF16),
            pltpu.SemaphoreType.REGULAR((3 + 2 * (groups - 1),)),
            dma((1,)),
            dma((here, groups)),
            dma((1,)),
            dma((here, groups)),
            dma((1,)),
            dma((here,)),
            dma((2,)),
            dma((groups, here)),
            dma((2,)),
            dma((2,)),
            dma((2,)),
            dma((1,)),
            dma((5,)),
        ],
        compiler_params=pltpu.CompilerParams(
            collective_id=0, has_side_effects=True, vmem_limit_bytes=32 * 1024 * 1024
        ),
        name="ladder",
    )(*[pltpu.with_memory_space_constraint(array, pltpu.HBM) for array in arrays])
    return jnp.transpose(result, (0, 3, 1, 2))


def solution(mesh):
    placed = (
        P("grp", "dev", None),
        P(None, "grp", None, "dev"),
        P(),
        P(),
        P("grp", "dev", None),
        P(),
    )
    groups, devs = mesh.shape["grp"], mesh.shape["dev"]

    def local(integrals, amplitudes, *rest):
        nef, vec, nij = amplitudes.shape[1:]
        nab = integrals.shape[1]
        square = devs == 2 * 2 * 2 and devs == 2 * groups
        packs = (
            2 * LANES < nef < 3 * LANES
            and 2 * (nef % LANES) == LANES
            and LANES < nab < 2 * LANES
            and vec * (nab % LANES) == LANES
            and nij % 8 == 0
            and (vec * nij) % 32 == 0
        )
        if square and packs:
            return fused(groups, integrals, amplitudes, *rest)
        return plain(integrals, amplitudes, *rest)

    return jax.shard_map(
        local, mesh=mesh, in_specs=placed, out_specs=P(None, "dev", None, "grp"), check_vma=False
    )
```

time: 36.6 us -> 33 us (0.902)
  the two profiles are of different devices: /device:TPU:0 before, /device:TPU:7 now
where the time goes in v2:
time: 33 us; the launch traced here: 32.9 us
  Pallas kernels  32 us (97%)
  local copies, waits for them, and re-layouts  0.88 us (3%)
    pallas_call x1, Pallas kernels, fused(): pl.pallas_call(functools.partial(body, dims), out_shape=jax.ShapeDtypeStr...  32 us
    unnamed x1, local copies, waits for them, and re-layouts  0.88 us

profile of v2, /device:TPU:7, one launch (start us, length us, event | category | flops | bytes accessed | tf_op | source)
XLA Modules:
  0.0 32.9 jit_solution(5285935332441940739)
XLA Ops:
  0.0 32.0 %ladder.1 = bf16[8,4,48,160]{3,2,1,0:T(8,128)(2,1)S(1)} custom-call(bf16[2,160,1280]{2,1,0:T(8,128)(2,1)} %ints_hbm.1, bf16[8,96,320]{2,1,0:T(8,128)(2,1)} %bitcast.7, f32[40]{0:T(128)} %occ_e_hbm.1, f32[280]{0:T(512)} %virt_e_hbm.1, s32[2,2,160]{2,1,0:T(2,128)} %bitcast.8, s32[2,192]{1,0:T(2,128)} %bitcast.9), custom_call_target="tpu_custom_call" | custom-call | tf_op jit(solution)/shard_map/ladder/pallas_call | solution.py:433
  32.0 0.9 %copy.8 = bf16[8,160,4,48]{1,3,2,0:T(8,128)(2,1)} copy(bf16[8,160,4,48]{1,3,2,0:T(8,128)(2,1)S(1)} %bitcast.6) | data formatting | bytes 983040

commit v3 on v2

--- a/solution.py
+++ b/solution.py
@@ -153,10 +153,13 @@
         at(z, jnp.where(swap, flip_x, flip_y), core),
     ]
     peers = [(partner, core == 0, 0), (x_peer, chip % 2 == 0, 1), (y_peer, chip < 2, 2)]
+    last = 3 + 2 * (groups - 1)
     for s in range(groups - 1):
         zz = reach(s)
         for c in range(2):
             peers.append((at(zz, chip, core if c == 0 else 1 - core), zz > z, 3 + s * 2 + c))
+    d_peer = at(z, diag, core)
+    peers.append((d_peer, chip < 2, last))
     barrier = pltpu.get_barrier_semaphore()
     for peer, higher, _ in peers:
         @pl.when(higher)
@@ -164,14 +167,14 @@
             pl.semaphore_signal(barrier, inc=1, device_id=peer, device_id_type=mesh_id)
     for load in loads + rest:
         load.start()
-    earlier = 2 * z + chip % 2 + chip // 2 + core
+    earlier = 2 * z + chip + core
 
     @pl.when(earlier > 0)
     def _():
         pl.semaphore_wait(barrier, earlier)
 
     for i, (peer, higher, slot) in enumerate(peers):
-        if i < 3:
+        if i < 3 or slot == last:
             there = slot
         else:
             s, c = (i - 3) // 2, (i - 3) % 2
@@ -182,6 +185,14 @@
         def _(peer=peer, there=there):
             pl.semaphore_signal(ready.at[there], inc=1, device_id=peer, device_id_type=mesh_id)
 
+    def met_z(name):
+        spot = outlets[name][1]
+        higher = outlets[name][0] > z
+
+        @pl.when(higher)
+        def _():
+            pl.semaphore_wait(ready.at[3 + 2 * spot], 1)
+
     def met(i):
         @pl.when(peers[i][1])
         def _():
@@ -211,13 +222,15 @@
     def left(ref, sem):
         whole(ref, sem).wait_send()
 
-    order = [(b, s) for s in (0, 1) for b in range(blocks_here)]
-    order += [(b, s) for b in range(blocks_here) for s in range(2, groups)]
-
-    def source(s):
-        if s < 2:
-            return z if s == 0 else z + 1 - 2 * (z % 2)
-        return across(s - 2)
+    near = z + 1 - 2 * (z % 2)
+    inner = jnp.logical_and(z > 0, z < groups - 1)
+    sources = {"O": (z, z), "N": (near, near), "C": (across(0),) * 2, "D": (across(1),) * 2}
+    turn = [
+        jnp.where(jnp.logical_or(z == groups - 1, jnp.logical_and(core == 0, z != 1)), 1, 0),
+        jnp.where(jnp.logical_and(core == 1, z == 1), 0, 1),
+    ]
+    sources["E"] = tuple(across(t) for t in turn)
+    sources["G"] = tuple(across(1 - t) for t in turn)
 
     def direct_main(b, way):
         for src, dst in bulk_parts(z * blocks_here + b, gath.at[b, z, chip]):
@@ -226,35 +239,43 @@
     def direct_tail(b, way):
         send(tails.at[b], gath.at[b, z, chip, bulk:chunk], d_send.at[0], d_recv.at[b, z], ways[way])
 
-    def inward_main(b, s):
-        to = reach(s)
+    skip = jnp.where(z == 2, 0, 1)
+    outlets = {"N": (near, 2 * (1 - skip)), "C": (across(0), skip), "D": (across(1), skip + 1)}
+
+    def inward_main(name, b):
+        to = outlets[name][0]
         for src, dst in bulk_parts(to * blocks_here + b, gath.at[b, z, chip]):
             send(src, dst, z_send.at[0], z_recv.at[b, z], at(to, chip, core))
 
-    def inward_tail(b, s):
-        to = reach(s)
+    def inward_tail(name, b):
+        to, spot = outlets[name]
         send(
-            tails.at[(s + 1) * blocks_here + b], gath.at[b, z, chip, bulk:chunk],
+            tails.at[(spot + 1) * blocks_here + b], gath.at[b, z, chip, bulk:chunk],
             z_send.at[0], z_recv.at[b, z], at(to, chip, core),
         )
 
-    def first(k):
-        b, s = order[k]
-        zz = source(s)
+    def first(name, b):
+        zz = sources[name][b]
         piece = gath.at[b, zz, chip]
         arrived(piece, z_recv.at[b, zz])
         for peer in (x_peer, y_peer):
             send(piece, piece, d_send.at[0], d_recv.at[b, zz], peer)
 
-    def second(k):
-        b, s = order[k]
-        zz = source(s)
+    def second(name, b):
+        zz = sources[name][b]
         arrived(gath.at[b, zz, 0:2], d_recv.at[b, zz])
         src = gath.at[b, zz, flip_x, 0:cut]
         send(src, src, f_send.at[0], f_recv.at[b], y_peer)
         src = gath.at[b, zz, flip_y, cut:chunk]
         send(src, src, f_send.at[0], f_recv.at[b], x_peer)
 
+    def cross(name, b):
+        piece = gath.at[b, sources[name][b], chip]
+        send(piece, piece, f_send.at[0], f_recv.at[b], d_peer)
+
+    def settled(name, b):
+        arrived(gath.at[b, sources[name][b], 0:2], d_recv.at[b, sources[name][b]])
+
     def third(b):
         arrived(gath.at[b, :, diag], f_recv.at[b])
 
@@ -266,33 +287,282 @@
     def loaded(slots, sem):
         pltpu.make_async_copy(amps.at[slots], amps.at[slots], sem).wait()
 
-    met_way(0)
-    direct_main(0, 0)
-    met_way(1)
-    direct_main(0, 1)
-    met(3)
-    inward_main(0, 0)
-    loaded(slice(0, blocks_here), load_amps.at[0])
-    for b in range(blocks_here):
-        pack(b)
-    for b in range(blocks_here):
-        if b > 0:
-            direct_main(b, 0)
-            direct_main(b, 1)
-        direct_tail(b, 0)
-        direct_tail(b, 1)
-    loaded(slice(blocks_here, groups * blocks_here), load_amps.at[1])
-    for slot in range(blocks_here, groups * blocks_here):
-        pack(slot)
-    inward_tail(0, 0)
-    for s in range(1, groups - 1):
-        met(3 + 2 * s)
-        inward_main(0, s)
-        inward_tail(0, s)
-    for b in range(1, blocks_here):
-        for s in range(groups - 1):
-            inward_main(b, s)
-            inward_tail(b, s)
+
+    @pl.when(chip == 3)
+    def _():
+        met_way(0)
+        direct_main(0, 0)
+        met_way(1)
+        direct_main(0, 1)
+
+        @pl.when(jnp.logical_not(inner))
+        def _():
+            met_z("N")
+            inward_main("N", 0)
+
+        loaded(slice(0, blocks_here), load_amps.at[0])
+        for b in range(blocks_here):
+            pack(b)
+        direct_tail(0, 0)
+        direct_tail(0, 1)
+        direct_main(1, 0)
+        direct_main(1, 1)
+        direct_tail(1, 0)
+        direct_tail(1, 1)
+        loaded(slice(blocks_here, groups * blocks_here), load_amps.at[1])
+        for slot in range(blocks_here, groups * blocks_here):
+            pack(slot)
+
+    @pl.when(jnp.logical_not(chip == 3))
+    def _():
+
+        @pl.when(jnp.logical_not(chip == 0))
+        def _():
+            met_way(0)
+            direct_main(0, 0)
+
+
+        @pl.when(jnp.logical_not(inner))
+        def _():
+            met_z("N")
+            inward_main("N", 0)
+
+        loaded(slice(0, blocks_here), load_amps.at[0])
+        for b in range(blocks_here):
+            pack(b)
+        loaded(slice(blocks_here, groups * blocks_here), load_amps.at[1])
+        for slot in range(blocks_here, groups * blocks_here):
+            pack(slot)
+
+        @pl.when(chip == 0)
+        def _():
+            met_way(0)
+            direct_main(0, 0)
+
+
+        @pl.when(jnp.logical_not(inner))
+        def _():
+            inward_tail("N", 0)
+
+        direct_tail(0, 0)
+        direct_main(1, 0)
+        direct_tail(1, 0)
+
+        @pl.when(inner)
+        def _():
+
+            @pl.when(z == 2)
+            def _():
+
+                @pl.when(core == 0)
+                def _():
+                    met_z("C")
+                    inward_main("C", 0)
+                    inward_tail("C", 0)
+                    met_z("D")
+                    inward_main("D", 0)
+                    inward_tail("D", 0)
+                    met_z("N")
+                    inward_main("N", 0)
+                    inward_tail("N", 0)
+                    inward_main("C", 1)
+                    inward_tail("C", 1)
+                    inward_main("D", 1)
+                    inward_tail("D", 1)
+                    inward_main("N", 1)
+                    inward_tail("N", 1)
+
+                @pl.when(jnp.logical_not(core == 0))
+                def _():
+                    met_z("C")
+                    inward_main("C", 0)
+                    inward_tail("C", 0)
+                    met_z("D")
+                    inward_main("D", 0)
+                    inward_tail("D", 0)
+                    met_z("N")
+                    inward_main("N", 0)
+                    inward_tail("N", 0)
+                    inward_main("C", 1)
+                    inward_tail("C", 1)
+                    inward_main("D", 1)
+                    inward_tail("D", 1)
+                    inward_main("N", 1)
+                    inward_tail("N", 1)
+
+
+            @pl.when(jnp.logical_not(z == 2))
+            def _():
+
+                @pl.when(core == 0)
+                def _():
+                    met_z("N")
+                    inward_main("N", 0)
+                    inward_tail("N", 0)
+                    met_z("C")
+                    inward_main("C", 0)
+                    inward_tail("C", 0)
+                    met_z("D")
+                    inward_main("D", 0)
+                    inward_tail("D", 0)
+                    inward_main("N", 1)
+                    inward_tail("N", 1)
+                    inward_main("C", 1)
+                    inward_tail("C", 1)
+                    inward_main("D", 1)
+                    inward_tail("D", 1)
+
+                @pl.when(jnp.logical_not(core == 0))
+                def _():
+                    met_z("N")
+                    inward_main("N", 0)
+                    inward_tail("N", 0)
+                    met_z("C")
+                    inward_main("C", 0)
+                    inward_tail("C", 0)
+                    met_z("D")
+                    inward_main("D", 0)
+                    inward_tail("D", 0)
+                    inward_main("N", 1)
+                    inward_tail("N", 1)
+                    inward_main("C", 1)
+                    inward_tail("C", 1)
+                    inward_main("D", 1)
+                    inward_tail("D", 1)
+
+
+        @pl.when(jnp.logical_not(inner))
+        def _():
+            met_z("C")
+            inward_main("C", 0)
+            inward_tail("C", 0)
+
+        met_way(1)
+        direct_main(0, 1)
+        direct_tail(0, 1)
+        direct_main(1, 1)
+        direct_tail(1, 1)
+
+
+    @pl.when(chip == 3)
+    def _():
+
+        @pl.when(inner)
+        def _():
+
+            @pl.when(z == 2)
+            def _():
+
+                @pl.when(core == 0)
+                def _():
+                    met_z("C")
+                    inward_main("C", 0)
+                    inward_tail("C", 0)
+                    met_z("D")
+                    inward_main("D", 0)
+                    inward_tail("D", 0)
+                    met_z("N")
+                    inward_main("N", 0)
+                    inward_tail("N", 0)
+                    inward_main("C", 1)
+                    inward_tail("C", 1)
+                    inward_main("D", 1)
+                    inward_tail("D", 1)
+                    inward_main("N", 1)
+                    inward_tail("N", 1)
+
+                @pl.when(jnp.logical_not(core == 0))
+                def _():
+                    met_z("C")
+                    inward_main("C", 0)
+                    inward_tail("C", 0)
+                    met_z("D")
+                    inward_main("D", 0)
+                    inward_tail("D", 0)
+                    met_z("N")
+                    inward_main("N", 0)
+                    inward_tail("N", 0)
+                    inward_main("C", 1)
+                    inward_tail("C", 1)
+                    inward_main("D", 1)
+                    inward_tail("D", 1)
+                    inward_main("N", 1)
+                    inward_tail("N", 1)
+
+
+            @pl.when(jnp.logical_not(z == 2))
+            def _():
+
+                @pl.when(core == 0)
+                def _():
+                    met_z("N")
+                    inward_main("N", 0)
+                    inward_tail("N", 0)
+                    met_z("C")
+                    inward_main("C", 0)
+                    inward_tail("C", 0)
+                    met_z("D")
+                    inward_main("D", 0)
+                    inward_tail("D", 0)
+                    inward_main("N", 1)
+                    inward_tail("N", 1)
+                    inward_main("C", 1)
+                    inward_tail("C", 1)
+                    inward_main("D", 1)
+                    inward_tail("D", 1)
+
+                @pl.when(jnp.logical_not(core == 0))
+                def _():
+                    met_z("N")
+                    inward_main("N", 0)
+                    inward_tail("N", 0)
+                    met_z("C")
+                    inward_main("C", 0)
+                    inward_tail("C", 0)
+                    met_z("D")
+                    inward_main("D", 0)
+                    inward_tail("D", 0)
+                    inward_main("N", 1)
+                    inward_tail("N", 1)
+                    inward_main("C", 1)
+                    inward_tail("C", 1)
+                    inward_main("D", 1)
+                    inward_tail("D", 1)
+
+
+        @pl.when(jnp.logical_not(inner))
+        def _():
+            inward_tail("N", 0)
+            met_z("C")
+            inward_main("C", 0)
+            inward_tail("C", 0)
+            met_z("D")
+            inward_main("D", 0)
+            inward_tail("D", 0)
+            inward_main("N", 1)
+            inward_tail("N", 1)
+            inward_main("C", 1)
+            inward_tail("C", 1)
+            inward_main("D", 1)
+            inward_tail("D", 1)
+
+
+    @pl.when(jnp.logical_not(chip == 3))
+    def _():
+
+        @pl.when(jnp.logical_not(inner))
+        def _():
+            met_z("D")
+            inward_main("D", 0)
+            inward_tail("D", 0)
+            inward_main("N", 1)
+            inward_tail("N", 1)
+            inward_main("C", 1)
+            inward_tail("C", 1)
+            inward_main("D", 1)
+            inward_tail("D", 1)
+
+
     met(0)
     send(vpairs_hbm, other_pairs, pair_send.at[0], pair_recv.at[0], partner)
     send(ints_hbm, other_ints, pair_send.at[1], pair_recv.at[1], partner)
@@ -373,35 +643,57 @@
             out[zz * blocks_here + b, v] = jnp.concatenate(pieces, axis=0).astype(BF16)
 
     prepare(0, ints, vpairs)
-    second(0)
-    first(2)
-    second(1)
+    second("O", 0)
+    first("N", 0)
+    second("O", 1)
     arrived(other_pairs, pair_recv.at[0])
     arrived(other_ints, pair_recv.at[1])
     prepare(1, other_ints, other_pairs)
-    first(3)
-    first(4)
-    second(2)
-    first(5)
-    second(4)
-    second(5)
+
+    @pl.when(inner)
+    def _():
+        first("E", 0)
+        first("G", 0)
+        second("N", 0)
+        first("N", 1)
+        second("E", 0)
+        first("E", 1)
+        second("G", 0)
+
+    @pl.when(jnp.logical_not(inner))
+    def _():
+        first("N", 1)
+        second("N", 0)
+        second("N", 1)
+        first("E", 0)
+        first("G", 0)
+        second("E", 0)
+        first("E", 1)
+        second("G", 0)
+
+    met(len(peers) - 1)
+    first("G", 1)
+    cross("G", 1)
     pltpu.make_async_copy(gath.at[:, z, chip, 0:bulk], gath.at[:, z, chip, 0:bulk], load_own.at[0]).wait()
     for s in range(groups - 1):
         met(4 + 2 * s)
+
+    @pl.when(inner)
+    def _():
+        second("N", 1)
+
     job(0, late[0])
     job(0, late[1])
-    first(6)
+    second("E", 1)
     job(0, late[2])
-    first(7)
-    second(3)
     third(0)
     job(0, late[3])
-    second(6)
-    second(7)
-    for i in range(groups - 1):
-        job(1, late[i])
+    settled("G", 1)
+    job(1, late[0])
+    job(1, late[1])
+    job(1, late[2])
     third(1)
-    job(1, late[groups - 1])
+    job(1, late[3])
 
     for b in range(blocks_here):
         arrived(recvbuf.at[z, b, 1 - core], o_recv.at[z, b])
@@ -451,7 +743,7 @@
             pltpu.VMEM((2 * chips * nij, LANES), F32),
             pltpu.VMEM((here, groups, 2, rows + nij, LANES), BF16),
             pltpu.VMEM((groups, here, 2, rows + nij, LANES), BF16),
-            pltpu.SemaphoreType.REGULAR((3 + 2 * (groups - 1),)),
+            pltpu.SemaphoreType.REGULAR((4 + 2 * (groups - 1),)),
             dma((1,)),
             dma((here, groups)),
             dma((1,)),

time: 33 us -> 30.7 us (0.930)
  the two profiles are of different devices: /device:TPU:7 before, /device:TPU:0 now
where the time goes in v3:
time: 30.7 us; the launch traced here: 30.5 us
  Pallas kernels  29.6 us (96%)
  local copies, waits for them, and re-layouts  0.88 us (3%)
    pallas_call x1, Pallas kernels, fused(): pl.pallas_call(functools.partial(body, dims), out_shape=jax.ShapeDtypeStr...  29.6 us
    unnamed x1, local copies, waits for them, and re-layouts  0.88 us

profile of v3, /device:TPU:0, one launch (start us, length us, event | category | flops | bytes accessed | tf_op | source)
XLA Modules:
  0.0 30.5 jit_solution(3624472381116420867)
XLA Ops:
  0.0 29.6 %ladder.1 = bf16[8,4,48,160]{3,2,1,0:T(8,128)(2,1)S(1)} custom-call(bf16[2,160,1280]{2,1,0:T(8,128)(2,1)} %ints_hbm.1, bf16[8,96,320]{2,1,0:T(8,128)(2,1)} %bitcast.7, f32[40]{0:T(128)} %occ_e_hbm.1, f32[280]{0:T(512)} %virt_e_hbm.1, s32[2,2,160]{2,1,0:T(2,128)} %bitcast.8, s32[2,192]{1,0:T(2,128)} %bitcast.9), custom_call_target="tpu_custom_call" | custom-call | tf_op jit(solution)/shard_map/ladder/pallas_call | solution.py:725
  29.6 0.9 %copy.8 = bf16[8,160,4,48]{1,3,2,0:T(8,128)(2,1)} copy(bf16[8,160,4,48]{1,3,2,0:T(8,128)(2,1)S(1)} %bitcast.6) | data formatting | bytes 983040

commit v4 on v3

--- a/solution.py
+++ b/solution.py
@@ -595,25 +595,32 @@
     lane = lax.broadcasted_iota(jnp.int32, (half, LANES), 1)
     main_lanes = nab // LANES * LANES
 
-    def job(b, p):
-        parts = []
-        for zz in range(groups):
-            end = gath[b, zz, p, bulk:chunk]
-            zero = jnp.zeros_like(end)
-            end2 = jnp.concatenate(
-                [jnp.where(lane < tail, end, zero), jnp.where(lane < tail, zero, end)], axis=0
-            )
-            parts += [gath[b, zz, p, i * rows : (i + 1) * rows] for i in range(main // LANES)] + [end2]
-        panel = jnp.concatenate(parts, axis=1)
+    def job(b, *columns):
+        panels = []
+        for p in columns:
+            parts = []
+            for zz in range(groups):
+                end = gath[b, zz, p, bulk:chunk]
+                zero = jnp.zeros_like(end)
+                end2 = jnp.concatenate(
+                    [jnp.where(lane < tail, end, zero), jnp.where(lane < tail, zero, end)], axis=0
+                )
+                parts += [gath[b, zz, p, i * rows : (i + 1) * rows] for i in range(main // LANES)] + [end2]
+            panels.append(jnp.concatenate(parts, axis=1))
+        panel = jnp.concatenate(panels, axis=0)
         for side in range(2):
             total = lax.dot_general(
                 panel, weights[b, side], (((1,), (1,)), ((), ())), preferred_element_type=F32
             )
-            scaled = total.reshape(vec, nij, nab) * recip[b, side, p][None]
-            ends = [scaled[v, :, main_lanes:nab] for v in range(vec)]
-            sendbuf[b, p, side, 0:rows, :] = scaled[:, :, 0:main_lanes].reshape(rows, main_lanes).astype(BF16)
-            sendbuf[b, p, side, rows : rows + nij, :] = jnp.concatenate(ends, axis=1).astype(BF16)
-
+            for i, p in enumerate(columns):
+                scaled = total[i * rows : (i + 1) * rows].reshape(vec, nij, nab) * recip[b, side, p][None]
+                ends = [scaled[v, :, main_lanes:nab] for v in range(vec)]
+                sendbuf[b, p, side, 0:rows, :] = scaled[:, :, 0:main_lanes].reshape(rows, main_lanes).astype(BF16)
+                sendbuf[b, p, side, rows : rows + nij, :] = jnp.concatenate(ends, axis=1).astype(BF16)
+        for p in columns:
+            deliver(b, p)
+
+    def deliver(b, p):
         @pl.when(p != z)
         def _():
             for side in range(2):
@@ -659,21 +666,42 @@
         second("E", 0)
         first("E", 1)
         second("G", 0)
+        met(len(peers) - 1)
+        first("G", 1)
+        cross("G", 1)
 
     @pl.when(jnp.logical_not(inner))
     def _():
-        first("N", 1)
-        second("N", 0)
-        second("N", 1)
-        first("E", 0)
-        first("G", 0)
-        second("E", 0)
-        first("E", 1)
-        second("G", 0)
-
-    met(len(peers) - 1)
-    first("G", 1)
-    cross("G", 1)
+
+        @pl.when(core == 0)
+        def _():
+            first("N", 1)
+            second("N", 0)
+            first("E", 0)
+            second("N", 1)
+            first("G", 0)
+            first("E", 1)
+            second("E", 0)
+            second("G", 0)
+            met(len(peers) - 1)
+            first("G", 1)
+            cross("G", 1)
+
+        @pl.when(jnp.logical_not(core == 0))
+        def _():
+            first("N", 1)
+            second("N", 0)
+            second("N", 1)
+            first("E", 0)
+            first("G", 0)
+            second("E", 0)
+            first("E", 1)
+            second("G", 0)
+            met(len(peers) - 1)
+            first("G", 1)
+            cross("G", 1)
+
+
     pltpu.make_async_copy(gath.at[:, z, chip, 0:bulk], gath.at[:, z, chip, 0:bulk], load_own.at[0]).wait()
     for s in range(groups - 1):
         met(4 + 2 * s)
@@ -682,16 +710,13 @@
     def _():
         second("N", 1)
 
-    job(0, late[0])
-    job(0, late[1])
+    job(0, late[0], late[1])
     second("E", 1)
     job(0, late[2])
     third(0)
     job(0, late[3])
     settled("G", 1)
-    job(1, late[0])
-    job(1, late[1])
-    job(1, late[2])
+    job(1, late[0], late[1], late[2])
     third(1)
     job(1, late[3])
 

time: 30.7 us -> 30.4 us (level)
  Pallas kernels: 29.6 us -> 29.2 us
    pallas_call x1, Pallas kernels: 29.6 us -> 29.2 us  [fused(): pl.pallas_call(functools.partial(body, dims), out_shape=jax.ShapeDtypeStr...]
where the time goes in v4:
time: 30.4 us; the launch traced here: 30.1 us
  Pallas kernels  29.2 us (96%)
  local copies, waits for them, and re-layouts  0.88 us (3%)
    pallas_call x1, Pallas kernels, fused(): pl.pallas_call(functools.partial(body, dims), out_shape=jax.ShapeDtypeStr...  29.2 us
    unnamed x1, local copies, waits for them, and re-layouts  0.88 us

profile of v4, /device:TPU:0, one launch (start us, length us, event | category | flops | bytes accessed | tf_op | source)
XLA Modules:
  0.0 30.1 jit_solution(8268590708364943549)
XLA Ops:
  0.0 29.2 %ladder.1 = bf16[8,4,48,160]{3,2,1,0:T(8,128)(2,1)S(1)} custom-call(bf16[2,160,1280]{2,1,0:T(8,128)(2,1)} %ints_hbm.1, bf16[8,96,320]{2,1,0:T(8,128)(2,1)} %bitcast.7, f32[40]{0:T(128)} %occ_e_hbm.1, f32[280]{0:T(512)} %virt_e_hbm.1, s32[2,2,160]{2,1,0:T(2,128)} %bitcast.8, s32[2,192]{1,0:T(2,128)} %bitcast.9), custom_call_target="tpu_custom_call" | custom-call | tf_op jit(solution)/shard_map/ladder/pallas_call | solution.py:750
  29.2 0.9 %copy.8 = bf16[8,160,4,48]{1,3,2,0:T(8,128)(2,1)} copy(bf16[8,160,4,48]{1,3,2,0:T(8,128)(2,1)S(1)} %bitcast.6) | data formatting | bytes 983040

commit v5 on v4

--- a/solution.py
+++ b/solution.py
@@ -649,8 +649,8 @@
                 pieces.append(jnp.concatenate([body_rows, end], axis=1))
             out[zz * blocks_here + b, v] = jnp.concatenate(pieces, axis=0).astype(BF16)
 
+    second("O", 0)
     prepare(0, ints, vpairs)
-    second("O", 0)
     first("N", 0)
     second("O", 1)
     arrived(other_pairs, pair_recv.at[0])
@@ -662,8 +662,8 @@
         first("E", 0)
         first("G", 0)
         second("N", 0)
+        second("E", 0)
         first("N", 1)
-        second("E", 0)
         first("E", 1)
         second("G", 0)
         met(len(peers) - 1)
@@ -705,12 +705,12 @@
     pltpu.make_async_copy(gath.at[:, z, chip, 0:bulk], gath.at[:, z, chip, 0:bulk], load_own.at[0]).wait()
     for s in range(groups - 1):
         met(4 + 2 * s)
+    job(0, late[0], late[1])
 
     @pl.when(inner)
     def _():
         second("N", 1)
 
-    job(0, late[0], late[1])
     second("E", 1)
     job(0, late[2])
     third(0)

time: 30.4 us -> 30.2 us (level)
  no operation moved by 1% of the time
where the time goes in v5:
time: 30.2 us; the launch traced here: 30 us
  Pallas kernels  29.1 us (96%)
  local copies, waits for them, and re-layouts  0.88 us (3%)
    pallas_call x1, Pallas kernels, fused(): pl.pallas_call(functools.partial(body, dims), out_shape=jax.ShapeDtypeStr...  29.1 us
    unnamed x1, local copies, waits for them, and re-layouts  0.88 us

profile of v5, /device:TPU:0, one launch (start us, length us, event | category | flops | bytes accessed | tf_op | source)
XLA Modules:
  0.0 30.0 jit_solution(10729083725919564935)
XLA Ops:
  0.0 29.1 %ladder.1 = bf16[8,4,48,160]{3,2,1,0:T(8,128)(2,1)S(1)} custom-call(bf16[2,160,1280]{2,1,0:T(8,128)(2,1)} %ints_hbm.1, bf16[8,96,320]{2,1,0:T(8,128)(2,1)} %bitcast.7, f32[40]{0:T(128)} %occ_e_hbm.1, f32[280]{0:T(512)} %virt_e_hbm.1, s32[2,2,160]{2,1,0:T(2,128)} %bitcast.8, s32[2,192]{1,0:T(2,128)} %bitcast.9), custom_call_target="tpu_custom_call" | custom-call | tf_op jit(solution)/shard_map/ladder/pallas_call | solution.py:750
  29.1 0.9 %copy.8 = bf16[8,160,4,48]{1,3,2,0:T(8,128)(2,1)} copy(bf16[8,160,4,48]{1,3,2,0:T(8,128)(2,1)S(1)} %bitcast.6) | data formatting | bytes 983040

commit v6 on v5

--- a/solution.py
+++ b/solution.py
@@ -652,10 +652,10 @@
     second("O", 0)
     prepare(0, ints, vpairs)
     first("N", 0)
-    second("O", 1)
     arrived(other_pairs, pair_recv.at[0])
     arrived(other_ints, pair_recv.at[1])
     prepare(1, other_ints, other_pairs)
+    second("O", 1)
 
     @pl.when(inner)
     def _():
@@ -706,12 +706,12 @@
     for s in range(groups - 1):
         met(4 + 2 * s)
     job(0, late[0], late[1])
+    second("E", 1)
 
     @pl.when(inner)
     def _():
         second("N", 1)
 
-    second("E", 1)
     job(0, late[2])
     third(0)
     job(0, late[3])

time: 30.2 us -> 30.3 us (level)
  no operation moved by 1% of the time
where the time goes in v6:
time: 30.3 us; the launch traced here: 30.1 us
  Pallas kernels  29.2 us (96%)
  local copies, waits for them, and re-layouts  0.88 us (3%)
    pallas_call x1, Pallas kernels, fused(): pl.pallas_call(functools.partial(body, dims), out_shape=jax.ShapeDtypeStr...  29.2 us
    unnamed x1, local copies, waits for them, and re-layouts  0.88 us

profile of v6, /device:TPU:0, one launch (start us, length us, event | category | flops | bytes accessed | tf_op | source)
XLA Modules:
  0.0 30.1 jit_solution(6910515172013650089)
XLA Ops:
  0.0 29.2 %ladder.1 = bf16[8,4,48,160]{3,2,1,0:T(8,128)(2,1)S(1)} custom-call(bf16[2,160,1280]{2,1,0:T(8,128)(2,1)} %ints_hbm.1, bf16[8,96,320]{2,1,0:T(8,128)(2,1)} %bitcast.7, f32[40]{0:T(128)} %occ_e_hbm.1, f32[280]{0:T(512)} %virt_e_hbm.1, s32[2,2,160]{2,1,0:T(2,128)} %bitcast.8, s32[2,192]{1,0:T(2,128)} %bitcast.9), custom_call_target="tpu_custom_call" | custom-call | tf_op jit(solution)/shard_map/ladder/pallas_call | solution.py:750
  29.2 0.9 %copy.8 = bf16[8,160,4,48]{1,3,2,0:T(8,128)(2,1)} copy(bf16[8,160,4,48]{1,3,2,0:T(8,128)(2,1)S(1)} %bitcast.6) | data formatting | bytes 983040

commit v7 on v6

--- a/solution.py
+++ b/solution.py
@@ -80,7 +80,6 @@
     z_recv,
     d_send,
     d_recv,
-    f_send,
     f_recv,
     o_send,
     o_recv,
@@ -153,11 +152,10 @@
         at(z, jnp.where(swap, flip_x, flip_y), core),
     ]
     peers = [(partner, core == 0, 0), (x_peer, chip % 2 == 0, 1), (y_peer, chip < 2, 2)]
-    last = 3 + 2 * (groups - 1)
+    last = 3 + groups - 1
     for s in range(groups - 1):
         zz = reach(s)
-        for c in range(2):
-            peers.append((at(zz, chip, core if c == 0 else 1 - core), zz > z, 3 + s * 2 + c))
+        peers.append((at(zz, chip, core), zz > z, 3 + s))
     d_peer = at(z, diag, core)
     peers.append((d_peer, chip < 2, last))
     barrier = pltpu.get_barrier_semaphore()
@@ -167,7 +165,7 @@
             pl.semaphore_signal(barrier, inc=1, device_id=peer, device_id_type=mesh_id)
     for load in loads + rest:
         load.start()
-    earlier = 2 * z + chip + core
+    earlier = z + chip + core
 
     @pl.when(earlier > 0)
     def _():
@@ -177,9 +175,8 @@
         if i < 3 or slot == last:
             there = slot
         else:
-            s, c = (i - 3) // 2, (i - 3) % 2
-            zz = reach(s)
-            there = 3 + c + 2 * jnp.where(z < zz, zz - 1 - z, z - 1)
+            zz = reach(i - 3)
+            there = 3 + jnp.where(z < zz, zz - 1 - z, z - 1)
 
         @pl.when(jnp.logical_not(higher))
         def _(peer=peer, there=there):
@@ -191,7 +188,7 @@
 
         @pl.when(higher)
         def _():
-            pl.semaphore_wait(ready.at[3 + 2 * spot], 1)
+            pl.semaphore_wait(ready.at[3 + spot], 1)
 
     def met(i):
         @pl.when(peers[i][1])
@@ -265,13 +262,13 @@
         zz = sources[name][b]
         arrived(gath.at[b, zz, 0:2], d_recv.at[b, zz])
         src = gath.at[b, zz, flip_x, 0:cut]
-        send(src, src, f_send.at[0], f_recv.at[b], y_peer)
+        send(src, src, d_send.at[0], f_recv.at[b], y_peer)
         src = gath.at[b, zz, flip_y, cut:chunk]
-        send(src, src, f_send.at[0], f_recv.at[b], x_peer)
+        send(src, src, d_send.at[0], f_recv.at[b], x_peer)
 
     def cross(name, b):
         piece = gath.at[b, sources[name][b], chip]
-        send(piece, piece, f_send.at[0], f_recv.at[b], d_peer)
+        send(piece, piece, d_send.at[0], f_recv.at[b], d_peer)
 
     def settled(name, b):
         arrived(gath.at[b, sources[name][b], 0:2], d_recv.at[b, sources[name][b]])
@@ -703,8 +700,6 @@
 
 
     pltpu.make_async_copy(gath.at[:, z, chip, 0:bulk], gath.at[:, z, chip, 0:bulk], load_own.at[0]).wait()
-    for s in range(groups - 1):
-        met(4 + 2 * s)
     job(0, late[0], late[1])
     second("E", 1)
 
@@ -728,8 +723,7 @@
             arrived(recvbuf.at[zz, b], o_recv.at[zz, b])
             unpack(zz, b)
     left(gath.at[:, 0 : groups - 1, 0], z_send.at[0])
-    left(gath.at[0], d_send.at[0])
-    left(gath.at[:, :, 0], f_send.at[0])
+    left(gath.at[:, 0 : groups - 1], d_send.at[0])
     left(sendbuf.at[:, 0 : groups - 1], o_send.at[0])
     left(sendbuf.at[:, 0, 0], o_send.at[1])
     left(other_pairs, pair_send.at[0])
@@ -768,12 +762,11 @@
             pltpu.VMEM((2 * chips * nij, LANES), F32),
             pltpu.VMEM((here, groups, 2, rows + nij, LANES), BF16),
             pltpu.VMEM((groups, here, 2, rows + nij, LANES), BF16),
-            pltpu.SemaphoreType.REGULAR((4 + 2 * (groups - 1),)),
+            pltpu.SemaphoreType.REGULAR((3 + groups,)),
             dma((1,)),
             dma((here, groups)),
             dma((1,)),
             dma((here, groups)),
-            dma((1,)),
             dma((here,)),
             dma((2,)),
             dma((groups, here)),

time: 30.3 us -> 30.2 us (level)
  no operation moved by 1% of the time
where the time goes in v7:
time: 30.2 us; the launch traced here: 30.1 us
  Pallas kernels  29.2 us (97%)
  local copies, waits for them, and re-layouts  0.88 us (3%)
    pallas_call x1, Pallas kernels, fused(): pl.pallas_call(functools.partial(body, dims), out_shape=jax.ShapeDtypeStr...  29.2 us
    unnamed x1, local copies, waits for them, and re-layouts  0.88 us

profile of v7, /device:TPU:0, one launch (start us, length us, event | category | flops | bytes accessed | tf_op | source)
XLA Modules:
  0.0 30.1 jit_solution(9294903879621611164)
XLA Ops:
  0.0 29.2 %ladder.1 = bf16[8,4,48,160]{3,2,1,0:T(8,128)(2,1)S(1)} custom-call(bf16[2,160,1280]{2,1,0:T(8,128)(2,1)} %ints_hbm.1, bf16[8,96,320]{2,1,0:T(8,128)(2,1)} %bitcast.7, f32[40]{0:T(128)} %occ_e_hbm.1, f32[280]{0:T(512)} %virt_e_hbm.1, s32[2,2,160]{2,1,0:T(2,128)} %bitcast.8, s32[2,192]{1,0:T(2,128)} %bitcast.9), custom_call_target="tpu_custom_call" | custom-call | tf_op jit(solution)/shard_map/ladder/pallas_call | solution.py:744
  29.2 0.9 %copy.8 = bf16[8,160,4,48]{1,3,2,0:T(8,128)(2,1)} copy(bf16[8,160,4,48]{1,3,2,0:T(8,128)(2,1)S(1)} %bitcast.6) | data formatting | bytes 983040
